TPU v7x, 512 devices: a whole 4x8x8 slice. The times are simulated.
512 devices in a mesh: section: 16 (over z_lo, x), peer: 32 (over z_hi, y, core).
Axes of the slice: x: 4, y: 8, z: 8 (z_hi: 2, z_lo: 4; z = z_hi * 4 + z_lo), core: 2. Of those that a mesh axis runs over, the one named last changes fastest.
Arguments:
- inbox: bfloat16 [16, 32, 128, 5120], P('section', 'peer'), may hold values from -6 to 6
- routes: int32 [16, 32, 32], replicated, may hold values from 0 to 1, as said below
- adapter_in: bfloat16 [16, 2, 16, 5120], P('section'), may hold values from -0.078125 to 0.078125
- adapter_out: bfloat16 [16, 2, 16, 5120], P('section'), may hold values from -1.5 to 1.5
- returned: bfloat16 [16, 32, 160, 5120], P('section', 'peer'), may hold values from -6 to 6
Outputs:
- handed: bfloat16 [16, 32, 160, 5120], P('section', 'peer')
- mean_in: float32 [16, 2, 16, 5120], P('section', None, None, 'peer')
- mean_out: float32 [16, 2, 16, 5120], P('section', None, None, 'peer')
Inputs may be any that keep to these rules, and one draw needn't show every extreme that they name: routes[s, p, q] is how many micro-batches peer p of section s sends to peer q of the next section; every row sums to 16; every column sums to at most 20, and in every section some column reaches 20; some entry of every section reaches 1.
All inputs are finite; a program needn't handle non-finite values.
Results may differ from a plain program's by a relative error of at most 0.015.
Values may be sent and summed in bfloat16 or wider, within the bound.
A program may use at most 64 MiB of HBM per device.

v0:
```python
import jax
import jax.numpy as jnp
from jax import lax
from jax.sharding import PartitionSpec as P

D = 5120
MB = 8


epsilon = 1e-06


def from_behind(array, axis, by):
    count = lax.axis_size(axis)
    return lax.ppermute(array, axis, [(i, (i + by) % count) for i in range(count)])


def in_blocks(array, dim, count):
    dims = array.shape
    blocks = array.reshape(*dims[:dim], count, dims[dim] // count, *dims[dim + 1 :])
    return jnp.moveaxis(blocks, dim, 0)


def sum_at_owner(array, axis, dim):
    blocks = in_blocks(array, dim, lax.axis_size(axis))
    arrived = lax.all_to_all(blocks, axis, split_axis=0, concat_axis=0, tiled=True)
    return arrived.astype(jnp.float32).sum(axis=0)


def in_one_piece(arrays, axis, dim, along):
    ends, at = ([], 0)
    for a in arrays[:-1]:
        at += a.shape[along]
        ends.append(at)
    both = jnp.concatenate(arrays, axis=along)
    return tuple(jnp.split(sum_at_owner(both, axis, dim), ends, axis=along))


def inverse_rms(hidden):
    return lax.rsqrt(jnp.mean(hidden * hidden, axis=-1, keepdims=True) + epsilon)


def contract_last(left, right):
    return lax.dot_general(
        left, right, (((1,), (1,)), ((), ())), preferred_element_type=jnp.float32
    )


def contract_first(left, right):
    return lax.dot_general(
        left, right, (((0,), (0,)), ((), ())), preferred_element_type=jnp.float32
    )


def section_forward(inputs, weight_in, weight_out):
    hidden = inputs.astype(jnp.float32)
    saved = []
    for layer in range(weight_in.shape[0]):
        scale = inverse_rms(hidden)
        plain = hidden * scale
        normed = plain.astype(jnp.bfloat16)
        lowered = contract_last(normed, weight_in[layer]).astype(jnp.bfloat16)
        saved.append((scale, plain, normed, lowered))
        hidden = hidden + jnp.dot(lowered, weight_out[layer], preferred_element_type=jnp.float32)
    return (hidden.astype(jnp.bfloat16), saved)


def section_backward(saved, weight_in, weight_out, incoming):
    grad = incoming.astype(jnp.float32)
    grads_in = []
    grads_out = []
    for layer in reversed(range(weight_in.shape[0])):
        scale, plain, normed, lowered = saved[layer]
        grad_bf = grad.astype(jnp.bfloat16)
        grads_out.append(contract_first(lowered, grad_bf))
        back_low = contract_last(grad_bf, weight_out[layer]).astype(jnp.bfloat16)
        grads_in.append(contract_first(back_low, normed))
        if layer > 0:
            spread = jnp.dot(back_low, weight_in[layer], preferred_element_type=jnp.float32)
            grad = grad + scale * (
                spread - plain * jnp.mean(spread * plain, axis=-1, keepdims=True)
            )
    return (jnp.stack(grads_in[::-1]), jnp.stack(grads_out[::-1]))


def sender_picks(row, peers, pair, micro):
    sent_end = jnp.cumsum(row)
    sent_start = sent_end - row
    index = jnp.arange(micro, dtype=jnp.int32)
    target = jnp.sum((sent_end[None, :] <= index[:, None]).astype(jnp.int32), axis=1)
    choose = target[:, None] == jnp.arange(peers, dtype=jnp.int32)[None, :]
    offset = index - jnp.sum(jnp.where(choose, sent_start[None, :], 0), axis=1)
    within = offset[:, None] == jnp.arange(pair, dtype=jnp.int32)[None, :]
    picks = choose[:, :, None] & within[:, None, :]
    return picks.reshape(micro, peers * pair).astype(jnp.bfloat16)


def receiver_places(column, peers, pair, capacity):
    slot_start = jnp.cumsum(column) - column
    position = jnp.arange(capacity, dtype=jnp.int32)
    within = jnp.arange(pair, dtype=jnp.int32)
    places = (position[:, None, None] == slot_start[None, :, None] + within[None, None, :]) & (
        within[None, None, :] < column[None, :, None]
    )
    return places.reshape(capacity, peers * pair).astype(jnp.bfloat16)


def route_forward(blocks, table, peer, peers, pair, capacity):
    micro = blocks.shape[0]
    row = lax.dynamic_index_in_dim(table, peer, 0, keepdims=False)
    column = lax.dynamic_index_in_dim(table, peer, 1, keepdims=False)
    picks = sender_picks(row, peers, pair, micro)
    outbound = jnp.einsum("jc,jrd->crd", picks, blocks, preferred_element_type=jnp.float32).astype(
        jnp.bfloat16
    )
    arrived = lax.all_to_all(outbound, "peer", split_axis=0, concat_axis=0, tiled=True)
    places = receiver_places(column, peers, pair, capacity)
    return jnp.einsum("kc,crd->krd", places, arrived, preferred_element_type=jnp.float32).astype(
        jnp.bfloat16
    )


def route_backward(slots, table, peer, peers, pair, micro):
    capacity = slots.shape[0]
    row = lax.dynamic_index_in_dim(table, peer, 0, keepdims=False)
    column = lax.dynamic_index_in_dim(table, peer, 1, keepdims=False)
    places = receiver_places(column, peers, pair, capacity)
    spread_out = jnp.einsum(
        "kc,krd->crd", places, slots, preferred_element_type=jnp.float32
    ).astype(jnp.bfloat16)
    arrived = lax.all_to_all(spread_out, "peer", split_axis=0, concat_axis=0, tiled=True)
    picks = sender_picks(row, peers, pair, micro)
    return jnp.einsum("jc,crd->jrd", picks, arrived, preferred_element_type=jnp.float32).astype(
        jnp.bfloat16
    )


def shards(inbox, routes, adapter_in, adapter_out, returned):
    peers = lax.axis_size("peer")
    section_count = lax.axis_size("section")
    section = lax.axis_index("section")
    peer = lax.axis_index("peer")
    tokens = inbox.shape[2]
    micro = tokens // MB
    pair = max(1, 2 * micro // peers)
    capacity = returned.shape[2] // MB
    weight_in = adapter_in[0]
    weight_out = adapter_out[0]
    earlier = lax.dynamic_index_in_dim(
        routes, (section + section_count - 1) % section_count, 0, keepdims=False
    )
    produced, saved = section_forward(inbox[0, 0], weight_in, weight_out)
    produced = produced.reshape(micro, MB, D)
    slots_here = returned[0, 0].reshape(capacity, MB, D)
    arrived_blocks = from_behind(produced, "section", 1)
    handed = route_forward(arrived_blocks, earlier, peer, peers, pair, capacity)
    gathered_back = route_backward(slots_here, earlier, peer, peers, pair, micro)
    incoming = from_behind(gathered_back, "section", -1)
    terms_in, terms_out = section_backward(
        saved, weight_in, weight_out, incoming.reshape(tokens, D)
    )
    summed_in, summed_out = in_one_piece(
        (terms_in.astype(jnp.bfloat16), terms_out.astype(jnp.bfloat16)), "peer", 2, 0
    )
    mean_in = summed_in / peers
    mean_out = summed_out / peers
    return (handed.reshape(1, 1, capacity * MB, D), mean_in[None], mean_out[None])


def solution(mesh):
    return jax.shard_map(
        shards,
        mesh=mesh,
        in_specs=(
            P("section", "peer", None, None),
            P(),
            P("section", None, None, None),
            P("section", None, None, None),
            P("section", "peer", None, None),
        ),
        out_specs=(
            P("section", "peer", None, None),
            P("section", None, None, "peer"),
            P("section", None, None, "peer"),
        ),
        check_vma=False,
    )
```

profile of v0, /device:TPU:7, one launch (start us, length us, event | category | flops | bytes accessed | tf_op | source)
XLA Modules:
  0.0 289.9 jit_solution(10939242299672325169)
XLA Ops:
  0.7 1.0 compare_reduce_fusion
  2.1 2.9 convolution_convert_fusion
  4.9 3.0 %copy.39 = bf16[32,8,5120]{2,1,0:T(8,128)(2,1)} copy(bf16[32,8,5120]{2,0,1:T(8,128)(2,1)S(1)} %convolution_convert_fusion) | data formatting | bytes 5242880 | tf_op jit(solution)/shard_map/convert_element_type | solution.py:130
  7.9 16.6 %all-to-all-start.1 = ((bf16[32,8,5120]{2,1,0:T(8,128)(2,1)}), bf16[32,8,5120]{2,1,0:T(8,128)(2,1)}, u32[]{:S(2)}, u32[]{:S(2)}) async-start(bf16[32,8,5120]{2,1,0:T(8,128)(2,1)} %copy.39), calls=%async_computation.1 | async-start | bytes 5242880 | tf_op jit(solution)/shard_map/all_to_all | solution.py:131
  24.9 1.5 fusion.22
  28.5 1.8 copy.34
  30.3 3.0 %collective-permute-start = (bf16[16,8,5120]{2,0,1:T(8,128)(2,1)}, bf16[16,8,5120]{2,0,1:T(8,128)(2,1)}, u32[]{:S(2)}, u32[]{:S(2)}) collective-permute-start(bf16[16,8,5120]{2,0,1:T(8,128)(2,1)} %copy.34), channel_id=1, source_target_pairs={{0,32},{32,64},{64,96},{96,128},{128,160},{160,192},{192,224},{224... | collective-permute-start | bytes 3932168 | tf_op jit(solution)/shard_map/ppermute | solution.py:15
  35.3 76.1 %collective-permute-done = bf16[16,8,5120]{2,0,1:T(8,128)(2,1)} collective-permute-done((bf16[16,8,5120]{2,0,1:T(8,128)(2,1)}, bf16[16,8,5120]{2,0,1:T(8,128)(2,1)}, u32[]{:S(2)}, u32[]{:S(2)}) %collective-permute-start) | collective-permute-done | bytes 1310752 | tf_op jit(solution)/shard_map/ppermute | solution.py:15
  111.4 2.3 convolution_convert_fusion.1
  113.6 2.9 %copy.35 = bf16[32,8,5120]{2,1,0:T(8,128)(2,1)} copy(bf16[32,8,5120]{2,0,1:T(8,128)(2,1)S(1)} %convolution_convert_fusion.1) | data formatting | bytes 5242880 | tf_op jit(solution)/shard_map/convert_element_type | solution.py:113
  116.6 13.1 %all-to-all-start = ((bf16[32,8,5120]{2,1,0:T(8,128)(2,1)}), bf16[32,8,5120]{2,1,0:T(8,128)(2,1)}, u32[]{:S(2)}, u32[]{:S(2)}) async-start(bf16[32,8,5120]{2,1,0:T(8,128)(2,1)} %copy.35), calls=%async_computation | async-start | bytes 5242880 | tf_op jit(solution)/shard_map/all_to_all | solution.py:116
  129.7 5.7 %convolution_convert_fusion.3 = bf16[16,8,5120]{2,0,1:T(8,128)(2,1)} fusion(bf16[32,8,5120]{2,1,0:T(8,128)(2,1)} %all-to-all-done.1, s32[16]{0:T(128)S(1)} %convert_reduce_fusion.1, pred[16]{0:T(512)(128)(4,1)S(1)} %subtract_compare_fusion), kind=kOutput, calls=%fused_computation.6 | convolution fusion | flops 42599424 | bytes 3932240 | tf_op jit(solution)/shard_map/jc,crd->jrd/dot_general | solution.py:133
  135.4 1.9 collective-permute-start.1
  137.3 1.4 fusion.13
  138.7 2.5 copy.42
  141.2 77.9 %collective-permute-done.1 = bf16[16,8,5120]{2,0,1:T(8,128)(2,1)} collective-permute-done((bf16[16,8,5120]{2,0,1:T(8,128)(2,1)}, bf16[16,8,5120]{2,0,1:T(8,128)(2,1)}, u32[]{:S(2)}, u32[]{:S(2)}) %collective-permute-start.1) | collective-permute-done | bytes 1310752 | tf_op jit(solution)/shard_map/ppermute | solution.py:15
  219.1 2.1 fusion.19
  221.2 2.5 multiply_reduce_fusion
  223.8 2.4 add_convert_fusion
  227.0 2.8 convolution_convert_fusion.5
  229.7 1.2 stack.4
  231.0 0.9 copy.44
  231.8 3.1 %copy.61 = bf16[16,8,5120]{2,1,0:T(8,128)(2,1)} copy(bf16[16,8,5120]{2,0,1:T(8,128)(2,1)} %collective-permute-done.1) | data formatting | bytes 2621440 | tf_op jit(solution)/shard_map/ppermute | solution.py:15
  234.9 2.4 copy.43
  237.4 2.8 fusion.18
  240.2 3.3 %fusion.17 = bf16[1,16,32,160]{3,1,2,0:T(8,128)(2,1)S(1)} fusion(bf16[32,160,128]{2,1,0:T(8,128)(2,1)} %bitcast.106, bf16[128,5120]{1,0:T(8,128)(2,1)S(1)} %add_convert_fusion, bf16[1,2,16,5120]{3,2,1,0:T(8,128)(2,1)} %param.8), kind=kOutput, calls=%fused_computation.34 | convolution fusion | flops 42027008 | bytes 2949120 | tf_op jit(solution)/shard_map/dot_general | solution.py:50
  243.4 1.3 maximum_bitcast_fusion
  244.7 1.2 copy.46
  245.9 12.7 %all-to-all-start.2 = ((bf16[32,4,16,160]{3,2,1,0:T(8,128)(2,1)}), bf16[32,4,16,160]{3,2,1,0:T(8,128)(2,1)S(1)}, u32[]{:S(2)}, u32[]{:S(2)}) async-start(bf16[32,4,16,160]{3,2,1,0:T(8,128)(2,1)} %copy.46), calls=%async_computation.2 | async-start | bytes 2097152 | tf_op jit(solution)/shard_map/all_to_all | solution.py:26
  258.7 4.7 %convolution_convert_fusion.2 = bf16[20,8,5120]{2,0,1:T(8,128)(2,1)S(1)} fusion(bf16[32,8,5120]{2,1,0:T(8,128)(2,1)} %all-to-all-done, s32[32]{0:T(128)S(1)} %subtract_reduce_fusion, pred[32]{0:T(512)(128)(4,1)S(1)} %get-tuple-element.3), kind=kOutput, calls=%fused_computation.2 | convolution fusion | flops 53249280 | bytes 4260000 | tf_op jit(solution)/shard_map/kc,crd->krd/dot_general | solution.py:118
  263.3 2.1 copy.60
  265.4 23.6 %all-to-all-done.2 = bf16[32,4,16,160]{3,2,1,0:T(8,128)(2,1)S(1)} async-done(((bf16[32,4,16,160]{3,2,1,0:T(8,128)(2,1)}), bf16[32,4,16,160]{3,2,1,0:T(8,128)(2,1)S(1)}, u32[]{:S(2)}, u32[]{:S(2)}) %all-to-all-start.2) | async-done | bytes 655392 | tf_op jit(solution)/shard_map/all_to_all | solution.py:26
  (38 shorter events, 6.5 us)
Async XLA Ops:
  0.6 1.5 copy-start
  7.9 16.6 %copy-start.3 = (bf16[1,1,128,5120]{3,2,1,0:T(8,128)(2,1)S(1)}, bf16[1,1,128,5120]{3,2,1,0:T(8,128)(2,1)}, u32[]{:S(2)}) copy-start(bf16[1,1,128,5120]{3,2,1,0:T(8,128)(2,1)} %param.5) | copy-start | bytes 3932164
  7.9 108.6 %all-to-all-start.1 = ((bf16[32,8,5120]{2,1,0:T(8,128)(2,1)}), bf16[32,8,5120]{2,1,0:T(8,128)(2,1)}, u32[]{:S(2)}, u32[]{:S(2)}) async-start(bf16[32,8,5120]{2,1,0:T(8,128)(2,1)} %copy.39), calls=%async_computation.1 | async-start | bytes 5242880 | tf_op jit(solution)/shard_map/all_to_all | solution.py:131
  24.5 1.9 copy-start.4
  24.8 2.2 copy-start.5
  27.0 1.5 copy-start.1
  30.3 81.1 %collective-permute-start = (bf16[16,8,5120]{2,0,1:T(8,128)(2,1)}, bf16[16,8,5120]{2,0,1:T(8,128)(2,1)}, u32[]{:S(2)}, u32[]{:S(2)}) collective-permute-start(bf16[16,8,5120]{2,0,1:T(8,128)(2,1)} %copy.34), channel_id=1, source_target_pairs={{0,32},{32,64},{64,96},{96,128},{128,160},{160,192},{192,224},{224... | collective-permute-start | bytes 3932168 | tf_op jit(solution)/shard_map/ppermute | solution.py:15
  116.6 129.3 %all-to-all-start = ((bf16[32,8,5120]{2,1,0:T(8,128)(2,1)}), bf16[32,8,5120]{2,1,0:T(8,128)(2,1)}, u32[]{:S(2)}, u32[]{:S(2)}) async-start(bf16[32,8,5120]{2,1,0:T(8,128)(2,1)} %copy.35), calls=%async_computation | async-start | bytes 5242880 | tf_op jit(solution)/shard_map/all_to_all | solution.py:116
  135.4 83.7 %collective-permute-start.1 = (bf16[16,8,5120]{2,0,1:T(8,128)(2,1)}, bf16[16,8,5120]{2,0,1:T(8,128)(2,1)}, u32[]{:S(2)}, u32[]{:S(2)}) collective-permute-start(bf16[16,8,5120]{2,0,1:T(8,128)(2,1)} %convolution_convert_fusion.3), channel_id=1, source_target_pairs={{0,480},{32,0},{64,32},{96,64},{128,96},{160,128},{192,160},{224,1... | collective-permute-start | bytes 3932168 | tf_op jit(solution)/shard_map/ppermute | solution.py:15
  138.7 82.6 %copy-start.6 = (bf16[1,2,16,5120]{3,2,1,0:T(8,128)(2,1)S(1)}, bf16[1,2,16,5120]{3,2,1,0:T(8,128)(2,1)}, u32[]{:S(2)}) copy-start(bf16[1,2,16,5120]{3,2,1,0:T(8,128)(2,1)} %param.7) | copy-start | bytes 983044
  221.2 2.5 copy-start.2
  245.9 43.2 %all-to-all-start.2 = ((bf16[32,4,16,160]{3,2,1,0:T(8,128)(2,1)}), bf16[32,4,16,160]{3,2,1,0:T(8,128)(2,1)S(1)}, u32[]{:S(2)}, u32[]{:S(2)}) async-start(bf16[32,4,16,160]{3,2,1,0:T(8,128)(2,1)} %copy.46), calls=%async_computation.2 | async-start | bytes 2097152 | tf_op jit(solution)/shard_map/all_to_all | solution.py:26
where the time goes:
time: 294 us; the launch traced here: 290 us
  waiting for transfers between devices  178 us (61%)
  starting transfers between devices  47.3 us (16%)
  matrix products  32.4 us (11%)
  local copies, waits for them, and re-layouts  23 us (8%)
  other arithmetic  8.66 us (3%)
    ppermute x2, waiting for transfers between devices, from_behind(): lax.ppermute(array, axis, [(i, (i + by) % count) for i in range(count)])  154 us
    all_to_all x1, waiting for transfers between devices, sum_at_owner(): lax.all_to_all(blocks, axis, split_axis=0, concat_axis=0, tiled=True)  23.6 us
    all_to_all x1, starting transfers between devices, route_backward(): lax.all_to_all(spread_out, 'peer', split_axis=0, concat_axis=0, tiled=True)  16.6 us
    all_to_all x1, starting transfers between devices, route_forward(): lax.all_to_all(outbound, 'peer', split_axis=0, concat_axis=0, tiled=True)  13.1 us
    all_to_all x1, starting transfers between devices, sum_at_owner(): lax.all_to_all(blocks, axis, split_axis=0, concat_axis=0, tiled=True)  12.7 us
    dot_general x4, matrix products, contract_first(): lax.dot_general(left, right, (((0,), (0,)), ((), ())), preferred_element_...  9.13 us
  transfers between devices with their start and end apart: 5, of which 3 were waited for; matrix products, arithmetic and copies ran while one was open for 19% of the time, Pallas kernels for 0%

commit v1 on v0

v1 whole, which is shorter than its diff:
```python
import jax
import jax.numpy as jnp
from jax import lax
from jax.experimental import pallas as pl
from jax.experimental.pallas import tpu as pltpu
from jax.sharding import PartitionSpec as P

MESH = pl.DeviceIdType.MESH
BF = jnp.bfloat16
F32 = jnp.float32

D = 5120
MB = 8
RANK = 16
SECTIONS = 16
PEERS = 32
ROWS_Y = 8
MICRO = 16
CAP = 20
TOK = CAP * MB
BLOCK = 32
CHUNK = 1024
WINDOW = 384
epsilon = 1e-06

STEPS = [(dy, dz, dc) for dy in (4, 3, 5, 2, 6, 1, 7, 0) for dz in (1, 0) for dc in (0, 1)]


def split_peer(peer):
    return peer // 16, (peer // 2) % ROWS_Y, peer % 2


def join_peer(z, y, c):
    return z * 16 + y * 2 + c


def route_kernel(
    pick, inbox, w_in, w_out, arrived, weights, staged, relay, s1, r1, s2, r2, sw, rw
):
    section = lax.axis_index("section")
    z, y, c = split_peer(lax.axis_index("peer"))
    ahead = (section + 1) % SECTIONS
    behind = (section + SECTIONS - 1) % SECTIONS
    in_plane = [(dy, dc) for dy in range(ROWS_Y) for dc in (0, 1) if dy or dc]

    barrier = pltpu.get_barrier_semaphore()
    for dz in (0, 1):
        pl.semaphore_signal(
            barrier,
            inc=1,
            device_id=(behind, join_peer((z + dz) % 2, y, c)),
            device_id_type=MESH,
        )
    for dy, dc in in_plane:
        pl.semaphore_signal(
            barrier,
            inc=1,
            device_id=(section, join_peer(z, (y + dy) % ROWS_Y, (c + dc) % 2)),
            device_id_type=MESH,
        )
    for i, (dy, dz, dc) in enumerate(STEPS):
        target = join_peer((z + dz) % 2, (y + dy) % ROWS_Y, (c + dc) % 2)
        staged[i] = inbox[pick[target]]
    pl.semaphore_wait(barrier, 2 + len(in_plane))

    def weight_hop(source):
        return pltpu.make_async_remote_copy(
            src_ref=source,
            dst_ref=weights.at[c],
            send_sem=sw.at[0],
            recv_sem=rw.at[0],
            device_id=(ahead, join_peer(z, y, c)),
            device_id_type=MESH,
        )

    def first_hop(i):
        return pltpu.make_async_remote_copy(
            src_ref=staged.at[i],
            dst_ref=relay.at[i],
            send_sem=s1.at[i],
            recv_sem=r1.at[i],
            device_id=(ahead, join_peer((z + STEPS[i][1]) % 2, y, c)),
            device_id_type=MESH,
        )

    def second_hop(i):
        dy, _, dc = STEPS[i]
        return pltpu.make_async_remote_copy(
            src_ref=relay.at[i],
            dst_ref=arrived.at[i],
            send_sem=s2.at[i],
            recv_sem=r2.at[i],
            device_id=(section, join_peer(z, (y + dy) % ROWS_Y, (c + dc) % 2)),
            device_id_type=MESH,
        )

    first = [first_hop(i) for i in range(len(STEPS))]
    second = [second_hop(i) if dy or dc else None for i, (dy, _, dc) in enumerate(STEPS)]
    for i in range(16):
        first[i].start()

    @pl.when(c == 0)
    def _():
        weight_hop(w_in).start()

    @pl.when(c == 1)
    def _():
        weight_hop(w_out).start()

    for i in range(16, len(STEPS)):
        first[i].start()

    share = pltpu.make_async_remote_copy(
        src_ref=weights.at[c],
        dst_ref=weights.at[c],
        send_sem=sw.at[1],
        recv_sem=rw.at[1],
        device_id=(section, join_peer(z, y, 1 - c)),
        device_id_type=MESH,
    )
    for i in range(len(STEPS)):
        first[i].wait_recv()
        if second[i] is None:
            arrived[i] = relay[i]
        else:
            second[i].start()
        if i == 23:
            weight_hop(w_in).wait_recv()
            share.start()
    for i in range(len(STEPS)):
        first[i].wait_send()
        if second[i] is not None:
            second[i].wait()
    weight_hop(w_in).wait_send()
    share.wait()


def route(pick, inbox, w_in, w_out):
    count = len(STEPS)
    slots = (count, MB, D)
    vmem = pl.BlockSpec(memory_space=pltpu.VMEM)
    return pl.pallas_call(
        route_kernel,
        out_shape=(
            jax.ShapeDtypeStruct(slots, BF),
            jax.ShapeDtypeStruct((2, 2, RANK, D), BF),
        ),
        in_specs=[pl.BlockSpec(memory_space=pltpu.SMEM), vmem, vmem, vmem],
        out_specs=(vmem, vmem),
        scratch_shapes=[
            pltpu.VMEM(slots, BF),
            pltpu.VMEM(slots, BF),
            pltpu.SemaphoreType.DMA((count,)),
            pltpu.SemaphoreType.DMA((count,)),
            pltpu.SemaphoreType.DMA((count,)),
            pltpu.SemaphoreType.DMA((count,)),
            pltpu.SemaphoreType.DMA((2,)),
            pltpu.SemaphoreType.DMA((2,)),
        ],
        compiler_params=pltpu.CompilerParams(
            collective_id=0, has_side_effects=True, vmem_limit_bytes=32 << 20
        ),
        name="route",
    )(pick, inbox, w_in, w_out)


def across(left, right):
    return lax.dot_general(left, right, (((1,), (1,)), ((), ())), preferred_element_type=F32)


def down(left, right):
    return lax.dot_general(left, right, (((0,), (0,)), ((), ())), preferred_element_type=F32)


def along(left, right):
    return jnp.dot(left, right, preferred_element_type=F32)


def mean_of(total):
    return jnp.sum(total, axis=-1, keepdims=True) / D


def section_kernel(
    source, taken, arrived, returned, weights, handed, terms, hid, n0, n1, g1, l0, l1, b0, b1
):
    pieces = [pl.ds(k, CHUNK) for k in range(0, D, CHUNK)]

    def block(step, carry):
        rows = pl.ds(pl.multiple_of(step * BLOCK, BLOCK), BLOCK)
        square = jnp.zeros((BLOCK, 1), F32)
        for piece in pieces:
            parts = []
            for k in range(BLOCK // MB):
                slot = step * (BLOCK // MB) + k
                part = arrived[source[slot], :, piece].astype(F32)
                parts.append(jnp.where(taken[slot] > 0, part, 0.0))
            x = jnp.concatenate(parts, axis=0)
            hid[:, piece] = x
            square += jnp.sum(x * x, axis=-1, keepdims=True)
        scale0 = lax.rsqrt(square / D + epsilon)
        low = jnp.zeros((BLOCK, RANK), F32)
        for piece in pieces:
            normed = (hid[:, piece] * scale0).astype(BF)
            n0[rows, piece] = normed
            low += across(normed, weights[0, 0, :, piece])
        low0 = low.astype(BF)
        l0[rows, :] = low0
        square = jnp.zeros((BLOCK, 1), F32)
        for piece in pieces:
            x = hid[:, piece] + along(low0, weights[1, 0, :, piece])
            hid[:, piece] = x
            square += jnp.sum(x * x, axis=-1, keepdims=True)
        scale1 = lax.rsqrt(square / D + epsilon)
        low = jnp.zeros((BLOCK, RANK), F32)
        back = jnp.zeros((BLOCK, RANK), F32)
        for piece in pieces:
            normed = (hid[:, piece] * scale1).astype(BF)
            n1[rows, piece] = normed
            low += across(normed, weights[0, 1, :, piece])
            back += across(returned[rows, piece], weights[1, 1, :, piece])
        low1 = low.astype(BF)
        back1 = back.astype(BF)
        l1[rows, :] = low1
        b1[rows, :] = back1
        both = jnp.zeros((BLOCK, 1), F32)
        for piece in pieces:
            x = hid[:, piece]
            handed[rows, piece] = (x + along(low1, weights[1, 1, :, piece])).astype(BF)
            spread = along(back1, weights[0, 1, :, piece])
            both += jnp.sum(spread * (x * scale1), axis=-1, keepdims=True)
        both = both / D
        back = jnp.zeros((BLOCK, RANK), F32)
        for piece in pieces:
            plain = hid[:, piece] * scale1
            spread = along(back1, weights[0, 1, :, piece])
            grad = returned[rows, piece].astype(F32) + scale1 * (spread - plain * both)
            grad = grad.astype(BF)
            g1[rows, piece] = grad
            back += across(grad, weights[1, 0, :, piece])
        b0[rows, :] = back.astype(BF)
        return carry

    lax.fori_loop(0, TOK // BLOCK, block, 0)
    for piece in pieces:
        terms[0:16, piece] = down(b0[...], n0[:, piece])
        terms[16:32, piece] = down(b1[...], n1[:, piece])
        terms[32:48, piece] = down(l0[...], g1[:, piece])
        terms[48:64, piece] = down(l1[...], returned[:, piece])


def section_step(source, taken, arrived, returned, weights):
    vmem = pl.BlockSpec(memory_space=pltpu.VMEM)
    smem = pl.BlockSpec(memory_space=pltpu.SMEM)
    return pl.pallas_call(
        section_kernel,
        out_shape=(
            jax.ShapeDtypeStruct((TOK, D), BF),
            jax.ShapeDtypeStruct((4 * RANK, D), F32),
        ),
        in_specs=[smem, smem, vmem, vmem, vmem],
        out_specs=(vmem, vmem),
        scratch_shapes=[
            pltpu.VMEM((BLOCK, D), F32),
            pltpu.VMEM((TOK, D), BF),
            pltpu.VMEM((TOK, D), BF),
            pltpu.VMEM((TOK, D), BF),
            pltpu.VMEM((TOK, RANK), BF),
            pltpu.VMEM((TOK, RANK), BF),
            pltpu.VMEM((TOK, RANK), BF),
            pltpu.VMEM((TOK, RANK), BF),
        ],
        compiler_params=pltpu.CompilerParams(vmem_limit_bytes=40 << 20),
        name="section_step",
    )(source, taken, arrived, returned, weights)


HALF = 2 * RANK
SPREAD = [(dy, dz) for dy in (4, 3, 5, 2, 6, 1, 7, 0) for dz in (1, 0)]


def reduce_kernel(terms, total, half, other_half, summed, landed, own, other, ss, rs, sc, rc):
    section = lax.axis_index("section")
    z, y, c = split_peer(lax.axis_index("peer"))
    ahead = (section + 1) % SECTIONS
    behind = (section + SECTIONS - 1) % SECTIONS
    partner = (section, join_peer(z, y, 1 - c))
    mine = pl.ds(pl.multiple_of(c * HALF, HALF), HALF)
    theirs = pl.ds(pl.multiple_of((1 - c) * HALF, HALF), HALF)

    barrier = pltpu.get_barrier_semaphore()
    pl.semaphore_signal(barrier, inc=1, device_id=partner, device_id_type=MESH)
    for dy, dz in SPREAD:
        pl.semaphore_signal(
            barrier,
            inc=1,
            device_id=(ahead, join_peer((z + dz) % 2, (y + dy) % ROWS_Y, c)),
            device_id_type=MESH,
        )
    half[...] = terms[theirs, :].astype(BF)
    pl.semaphore_wait(barrier, 1 + len(SPREAD))

    to_core = pltpu.make_async_remote_copy(
        src_ref=half,
        dst_ref=other_half,
        send_sem=sc.at[0],
        recv_sem=rc.at[0],
        device_id=partner,
        device_id_type=MESH,
    )
    to_core.start()
    to_core.wait()
    summed[...] = (terms[mine, :] + other_half[...].astype(F32)).astype(BF)
    copies = []
    for i, (dy, dz) in enumerate(SPREAD):
        chip_z, chip_y = (z + dz) % 2, (y + dy) % ROWS_Y
        start = pl.multiple_of(128 * ((5 * (chip_z * ROWS_Y + chip_y)) // 2), 128)
        copy = pltpu.make_async_remote_copy(
            src_ref=summed.at[:, pl.ds(start, WINDOW)],
            dst_ref=landed.at[i],
            send_sem=ss.at[i],
            recv_sem=rs.at[i],
            device_id=(behind, join_peer(chip_z, chip_y, c)),
            device_id_type=MESH,
        )
        copy.start()
        copies.append(copy)
    for copy in copies:
        copy.wait()
    own[...] = jnp.sum(landed[...].astype(F32), axis=0)
    back = pltpu.make_async_remote_copy(
        src_ref=own,
        dst_ref=other,
        send_sem=sc.at[1],
        recv_sem=rc.at[1],
        device_id=partner,
        device_id_type=MESH,
    )
    back.start()
    back.wait()
    total[mine, :] = own[...] / PEERS
    total[theirs, :] = other[...] / PEERS


def reduce_terms(terms):
    vmem = pl.BlockSpec(memory_space=pltpu.VMEM)
    count = len(SPREAD)
    return pl.pallas_call(
        reduce_kernel,
        out_shape=jax.ShapeDtypeStruct((2 * HALF, WINDOW), F32),
        in_specs=[vmem],
        out_specs=vmem,
        scratch_shapes=[
            pltpu.VMEM((HALF, D), BF),
            pltpu.VMEM((HALF, D), BF),
            pltpu.VMEM((HALF, D), BF),
            pltpu.VMEM((count, HALF, WINDOW), BF),
            pltpu.VMEM((HALF, WINDOW), F32),
            pltpu.VMEM((HALF, WINDOW), F32),
            pltpu.SemaphoreType.DMA((count,)),
            pltpu.SemaphoreType.DMA((count,)),
            pltpu.SemaphoreType.DMA((2,)),
            pltpu.SemaphoreType.DMA((2,)),
        ],
        compiler_params=pltpu.CompilerParams(
            collective_id=1, has_side_effects=True, vmem_limit_bytes=32 << 20
        ),
        name="reduce_terms",
    )(terms)


def tables(routes, section, peer):
    row = lax.dynamic_index_in_dim(
        lax.dynamic_index_in_dim(routes, section, 0, keepdims=False), peer, 0, keepdims=False
    )
    behind = (section + SECTIONS - 1) % SECTIONS
    column = lax.dynamic_index_in_dim(
        lax.dynamic_index_in_dim(routes, behind, 0, keepdims=False), peer, 1, keepdims=False
    )
    index = jnp.arange(PEERS, dtype=jnp.int32)
    before = index[None, :] < index[:, None]
    pick = jnp.minimum(jnp.sum(jnp.where(before, row[None, :], 0), axis=1), MICRO - 1)
    slot = jnp.sum(jnp.where(before, column[None, :], 0), axis=1)
    z, y, c = split_peer(peer)
    from_z, from_y, from_c = split_peer(index)
    turn = (y - from_y + ROWS_Y) % ROWS_Y
    place = jnp.sum(
        jnp.where(
            turn[:, None] == jnp.asarray([4, 3, 5, 2, 6, 1, 7, 0], jnp.int32)[None, :],
            jnp.arange(ROWS_Y, dtype=jnp.int32)[None, :],
            0,
        ),
        axis=1,
    )
    step = place * 4 + jnp.where(from_z == z, 2, 0) + jnp.where(from_c == c, 0, 1)
    here = (jnp.arange(CAP, dtype=jnp.int32)[:, None] == slot[None, :]) & (column[None, :] > 0)
    source = jnp.sum(jnp.where(here, step[None, :], 0), axis=1)
    taken = jnp.sum(here.astype(jnp.int32), axis=1)
    return pick, source, taken


def shards(inbox, routes, adapter_in, adapter_out, returned):
    section = lax.axis_index("section")
    peer = lax.axis_index("peer")
    pick, source, taken = tables(routes, section, peer)
    arrived, weights = route(
        pick, inbox.reshape(MICRO, MB, D), adapter_in[0], adapter_out[0]
    )
    handed, terms = section_step(source, taken, arrived, returned[0, 0], weights)
    total = reduce_terms(terms)
    start = (peer // 2 % 2) * 64 + (peer % 2) * 160
    own = lax.dynamic_slice_in_dim(total, start, D // PEERS, axis=1).reshape(2, 2, RANK, D // PEERS)
    return handed[None, None], own[0][None], own[1][None]


def solution(mesh):
    return jax.shard_map(
        shards,
        mesh=mesh,
        in_specs=(
            P("section", "peer", None, None),
            P(),
            P("section", None, None, None),
            P("section", None, None, None),
            P("section", "peer", None, None),
        ),
        out_specs=(
            P("section", "peer", None, None),
            P("section", None, None, "peer"),
            P("section", None, None, "peer"),
        ),
        check_vma=False,
    )
```

time: 294 us -> 180 us (0.61)
  the two profiles are of different devices: /device:TPU:7 before, /device:TPU:193 now
where the time goes in v1:
time: 180 us
  Pallas kernels  173 us (96%)
  local copies, waits for them, and re-layouts  5.03 us (3%)
    pallas_call x1, Pallas kernels, route(): pl.pallas_call(route_kernel, out_shape=(jax.ShapeDtypeStruct(slots, BF),...  136 us
    pallas_call x1, Pallas kernels, reduce_terms(): pl.pallas_call(reduce_kernel, out_shape=jax.ShapeDtypeStruct((2 * HALF, W...  25.1 us
    pallas_call x1, Pallas kernels, section_step(): pl.pallas_call(section_kernel, out_shape=(jax.ShapeDtypeStruct((TOK, D),...  11.4 us
    unnamed x10, local copies, waits for them, and re-layouts  4.12 us

profile of v1, /device:TPU:193, one launch (start us, length us, event | category | flops | bytes accessed | tf_op | source)
XLA Modules:
  0.0 179.7 jit_solution(13690356761332433412)
XLA Ops:
  0.6 0.0 copy-start
  0.6 0.0 copy-start.1
  0.7 0.8 copy-done
  1.6 0.2 dynamic-slice_reduce_fusion
  1.8 0.1 select_reduce_fusion
  1.9 0.7 select_reduce_fusion.3
  2.7 0.1 select_reduce_fusion.1
  2.8 0.1 convert_reduce_fusion
  2.9 0.0 copy-start.2
  2.9 1.3 copy-done.2
  4.2 0.0 copy-start.3
  4.2 1.0 copy-done.3
  5.2 0.0 copy-start.4
  5.2 1.0 copy-done.4
  6.2 136.2 %route.1 = (bf16[32,8,5120]{2,1,0:T(8,128)(2,1)S(1)}, bf16[2,2,16,5120]{3,2,1,0:T(8,128)(2,1)S(1)}) custom-call(s32[32]{0:T(128)S(1)} %broadcast_minimum_fusion.pick, bf16[16,8,5120]{2,1,0:T(8,128)(2,1)S(1)} %bitcast.10, bf16[2,16,5120]{2,1,0:T(8,128)(2,1)S(1)} %bitcast.11, bf16[2,16,5120]{2,1,0:T(8,128)(2,1)S(1)} %bitcast.12), custom_call_target="tpu_custom_call" | custom-call | tf_op jit(solution)/shard_map/route/pallas_call | solution.py:142
  142.4 0.0 copy-done.1
  142.4 11.4 %section_step.1 = (bf16[160,5120]{1,0:T(8,128)(2,1)}, f32[64,5120]{1,0:T(8,128)S(1)}) custom-call(s32[20]{0:T(128)S(1)} %get-tuple-element.12.source, s32[20]{0:T(128)S(1)} %get-tuple-element.11.taken, bf16[32,8,5120]{2,1,0:T(8,128)(2,1)S(1)} %get-tuple-element.7.arrived, bf16[160,5120]{1,0:T(8,128)(2,1)S(1)} %bitcast.9, ...), custom_call_target="tpu_custom_call" | custom-call | tf_op jit(solution)/shard_map/section_step/pallas_call | solution.py:254
  153.8 25.1 %reduce_terms.1 = f32[64,384]{1,0:T(8,128)S(1)} custom-call(f32[64,5120]{1,0:T(8,128)S(1)} %get-tuple-element.10.terms), custom_call_target="tpu_custom_call" | custom-call | tf_op jit(solution)/shard_map/reduce_terms/pallas_call | solution.py:347
  179.0 0.7 fusion.8
  (5 shorter events, 0.0 us)
Async XLA Ops:
  0.6 1.0 copy-start
  0.6 141.7 %copy-start.1 = (bf16[1,1,160,5120]{3,2,1,0:T(8,128)(2,1)S(1)}, bf16[1,1,160,5120]{3,2,1,0:T(8,128)(2,1)}, u32[]{:S(2)}) copy-start(bf16[1,1,160,5120]{3,2,1,0:T(8,128)(2,1)} %param.10) | copy-start | bytes 4915204
  2.9 1.3 copy-start.2
  4.2 1.0 copy-start.3
  5.2 1.0 copy-start.4

commit v2 on v1

--- a/solution.py
+++ b/solution.py
@@ -23,139 +23,203 @@
 WINDOW = 384
 epsilon = 1e-06
 
-STEPS = [(dy, dz, dc) for dy in (4, 3, 5, 2, 6, 1, 7, 0) for dz in (1, 0) for dc in (0, 1)]
-
-
-def split_peer(peer):
-    return peer // 16, (peer // 2) % ROWS_Y, peer % 2
-
-
-def join_peer(z, y, c):
-    return z * 16 + y * 2 + c
+SLOTS = [(dy, dc) for dy in (4, 3, 5, 2, 6, 1, 7, 0) for dc in (0, 1)]
+FAR = len(SLOTS)
+SPLIT = 4
+LAG = 4
+
+
+def place_of(section, peer):
+    z = (peer // 16) * 4 + section // 4
+    return section % 4, (peer // 2) % ROWS_Y, z, peer % 2
+
+
+def device_at(x, y, z, c):
+    z = (z + 8) % 8
+    return (z % 4) * 4 + (x + 4) % 4, (z // 4) * 16 + ((y + ROWS_Y) % ROWS_Y) * 2 + c
 
 
 def route_kernel(
-    pick, inbox, w_in, w_out, arrived, weights, staged, relay, s1, r1, s2, r2, sw, rw
+    pick, inbox, w_in, w_out, arrived, weights, mine, staged, relay, middle, load, s1, r1, s2, r2, s3, s4, r3, sw, rw
 ):
-    section = lax.axis_index("section")
-    z, y, c = split_peer(lax.axis_index("peer"))
-    ahead = (section + 1) % SECTIONS
-    behind = (section + SECTIONS - 1) % SECTIONS
+    x, y, z, c = place_of(lax.axis_index("section"), lax.axis_index("peer"))
+    leaving, entering = x == 3, x == 0
+    shift_out, shift_in = jnp.where(leaving, 1, 0), jnp.where(entering, 1, 0)
     in_plane = [(dy, dc) for dy in range(ROWS_Y) for dc in (0, 1) if dy or dc]
 
+    fetch = pltpu.make_async_copy(inbox, mine, load)
+    fetch.start()
     barrier = pltpu.get_barrier_semaphore()
-    for dz in (0, 1):
-        pl.semaphore_signal(
-            barrier,
-            inc=1,
-            device_id=(behind, join_peer((z + dz) % 2, y, c)),
+
+    def greet(*where):
+        pl.semaphore_signal(barrier, inc=1, device_id=device_at(*where), device_id_type=MESH)
+
+    greet(x - 1, y, z - shift_in, c)
+    greet(x - 1, y, z - shift_in - 4, c)
+
+    @pl.when(entering)
+    def _():
+        greet(x - 1, y, z - 3, c)
+        greet(x, y, z - 2, c)
+
+    for dy, dc in in_plane:
+        greet(x, y + dy, z, (c + dc) % 2)
+    fetch.wait()
+    for k, (dy, dc) in enumerate(SLOTS):
+        for far in (1, 0):
+            target = device_at(x + 1, y + dy, z + shift_out + 4 * far, (c + dc) % 2)[1]
+            staged[k + FAR * (1 - far)] = mine[pick[target]]
+    greeted = 2 + len(in_plane) + shift_out + shift_in
+    pl.semaphore_wait(barrier, greeted)
+
+    def send(source, target, send_sem, recv_sem, *where):
+        return pltpu.make_async_remote_copy(
+            src_ref=source,
+            dst_ref=target,
+            send_sem=send_sem,
+            recv_sem=recv_sem,
+            device_id=device_at(*where),
             device_id_type=MESH,
         )
-    for dy, dc in in_plane:
-        pl.semaphore_signal(
-            barrier,
-            inc=1,
-            device_id=(section, join_peer(z, (y + dy) % ROWS_Y, (c + dc) % 2)),
-            device_id_type=MESH,
+
+    def weight_hop(source):
+        return send(source, weights.at[c], sw.at[0], rw.at[0], x + 1, y, z + shift_out, c)
+
+    near, far, outward, onward, final = [], [], [], [], []
+    for k in range(FAR):
+        far.append(
+            send(
+                staged.at[k], relay.at[k], s2.at[k], r2.at[k],
+                x + 1, y, z + shift_out + 4, c,
+            )
         )
-    for i, (dy, dz, dc) in enumerate(STEPS):
-        target = join_peer((z + dz) % 2, (y + dy) % ROWS_Y, (c + dc) % 2)
-        staged[i] = inbox[pick[target]]
-    pl.semaphore_wait(barrier, 2 + len(in_plane))
-
-    def weight_hop(source):
-        return pltpu.make_async_remote_copy(
-            src_ref=source,
-            dst_ref=weights.at[c],
-            send_sem=sw.at[0],
-            recv_sem=rw.at[0],
-            device_id=(ahead, join_peer(z, y, c)),
-            device_id_type=MESH,
+        near.append(
+            send(
+                staged.at[FAR + k], relay.at[FAR + k], s2.at[FAR + k], r2.at[FAR + k],
+                x + 1, y, z + shift_out, c,
+            )
         )
-
-    def first_hop(i):
-        return pltpu.make_async_remote_copy(
-            src_ref=staged.at[i],
-            dst_ref=relay.at[i],
-            send_sem=s1.at[i],
-            recv_sem=r1.at[i],
-            device_id=(ahead, join_peer((z + STEPS[i][1]) % 2, y, c)),
-            device_id_type=MESH,
+    for k in range(SPLIT):
+        outward.append(
+            send(staged.at[k], middle.at[k], s1.at[k], r1.at[k], x + 1, y, z + 3, c)
         )
-
-    def second_hop(i):
-        dy, _, dc = STEPS[i]
-        return pltpu.make_async_remote_copy(
-            src_ref=relay.at[i],
-            dst_ref=arrived.at[i],
-            send_sem=s2.at[i],
-            recv_sem=r2.at[i],
-            device_id=(section, join_peer(z, (y + dy) % ROWS_Y, (c + dc) % 2)),
-            device_id_type=MESH,
-        )
-
-    first = [first_hop(i) for i in range(len(STEPS))]
-    second = [second_hop(i) if dy or dc else None for i, (dy, _, dc) in enumerate(STEPS)]
-    for i in range(16):
-        first[i].start()
-
-    @pl.when(c == 0)
-    def _():
-        weight_hop(w_in).start()
-
-    @pl.when(c == 1)
-    def _():
-        weight_hop(w_out).start()
-
-    for i in range(16, len(STEPS)):
-        first[i].start()
-
-    share = pltpu.make_async_remote_copy(
-        src_ref=weights.at[c],
-        dst_ref=weights.at[c],
-        send_sem=sw.at[1],
-        recv_sem=rw.at[1],
-        device_id=(section, join_peer(z, y, 1 - c)),
-        device_id_type=MESH,
-    )
-    for i in range(len(STEPS)):
-        first[i].wait_recv()
-        if second[i] is None:
+        onward.append(send(middle.at[k], relay.at[k], s3.at[k], r2.at[k], x, y, z + 2, c))
+    for i in range(2 * FAR):
+        dy, dc = SLOTS[i % FAR]
+        if dy or dc:
+            final.append(
+                send(
+                    relay.at[i], arrived.at[i], s4.at[i], r3.at[i],
+                    x, y + dy, z, (c + dc) % 2,
+                )
+            )
+        else:
+            final.append(None)
+
+    def pass_on(i):
+        if final[i] is None:
             arrived[i] = relay[i]
         else:
-            second[i].start()
-        if i == 23:
+            final[i].start()
+
+    @pl.when(leaving)
+    def _():
+        for k in range(SPLIT):
+            outward[k].start()
+
+    for k in range(FAR):
+        if k < SPLIT:
+
+            @pl.when(jnp.logical_not(leaving))
+            def _():
+                far[k].start()
+        else:
+            far[k].start()
+        near[k].start()
+        if k == FAR // 2:
+
+            @pl.when(c == 0)
+            def _():
+                weight_hop(w_in).start()
+
+            @pl.when(c == 1)
+            def _():
+                weight_hop(w_out).start()
+
+    share = send(weights.at[c], weights.at[c], sw.at[1], rw.at[1], x, y, z, 1 - c)
+    order = list(range(SPLIT, FAR))
+    order = order[:SPLIT] + list(range(SPLIT)) + order[SPLIT:]
+    for t in range(FAR + LAG):
+        if t < FAR:
+            near[t].wait_recv()
+            pass_on(FAR + t)
+        if t < SPLIT:
+
+            @pl.when(entering)
+            def _():
+                outward[t].wait_recv()
+                onward[t].start()
+        if t == FAR - 2:
             weight_hop(w_in).wait_recv()
             share.start()
-    for i in range(len(STEPS)):
-        first[i].wait_send()
-        if second[i] is not None:
-            second[i].wait()
+        if t >= LAG:
+            far[order[t - LAG]].wait_recv()
+            pass_on(order[t - LAG])
+    for k in range(FAR):
+        near[k].wait_send()
+        if k >= SPLIT:
+            far[k].wait_send()
+
+    @pl.when(leaving)
+    def _():
+        for copy in outward:
+            copy.wait_send()
+
+    @pl.when(jnp.logical_not(leaving))
+    def _():
+        for copy in far[:SPLIT]:
+            copy.wait_send()
+
+    @pl.when(entering)
+    def _():
+        for copy in onward:
+            copy.wait_send()
+
+    for copy in final:
+        if copy is not None:
+            copy.wait()
     weight_hop(w_in).wait_send()
     share.wait()
 
 
 def route(pick, inbox, w_in, w_out):
-    count = len(STEPS)
-    slots = (count, MB, D)
+    slots = (2 * FAR, MB, D)
     vmem = pl.BlockSpec(memory_space=pltpu.VMEM)
+    anywhere = pl.BlockSpec(memory_space=pl.ANY)
+    dma = pltpu.SemaphoreType.DMA
     return pl.pallas_call(
         route_kernel,
         out_shape=(
             jax.ShapeDtypeStruct(slots, BF),
             jax.ShapeDtypeStruct((2, 2, RANK, D), BF),
         ),
-        in_specs=[pl.BlockSpec(memory_space=pltpu.SMEM), vmem, vmem, vmem],
+        in_specs=[pl.BlockSpec(memory_space=pltpu.SMEM), anywhere, anywhere, anywhere],
         out_specs=(vmem, vmem),
         scratch_shapes=[
+            pltpu.VMEM((MICRO, MB, D), BF),
             pltpu.VMEM(slots, BF),
             pltpu.VMEM(slots, BF),
-            pltpu.SemaphoreType.DMA((count,)),
-            pltpu.SemaphoreType.DMA((count,)),
-            pltpu.SemaphoreType.DMA((count,)),
-            pltpu.SemaphoreType.DMA((count,)),
-            pltpu.SemaphoreType.DMA((2,)),
-            pltpu.SemaphoreType.DMA((2,)),
+            pltpu.VMEM((SPLIT, MB, D), BF),
+            dma(()),
+            dma((SPLIT,)),
+            dma((SPLIT,)),
+            dma((2 * FAR,)),
+            dma((2 * FAR,)),
+            dma((SPLIT,)),
+            dma((2 * FAR,)),
+            dma((2 * FAR,)),
+            dma((2,)),
+            dma((2,)),
         ],
         compiler_params=pltpu.CompilerParams(
             collective_id=0, has_side_effects=True, vmem_limit_bytes=32 << 20
@@ -274,6 +338,14 @@
     )(source, taken, arrived, returned, weights)
 
 
+def split_peer(peer):
+    return peer // 16, (peer // 2) % ROWS_Y, peer % 2
+
+
+def join_peer(z, y, c):
+    return z * 16 + y * 2 + c
+
+
 HALF = 2 * RANK
 SPREAD = [(dy, dz) for dy in (4, 3, 5, 2, 6, 1, 7, 0) for dz in (1, 0)]
 
@@ -380,18 +452,18 @@
     before = index[None, :] < index[:, None]
     pick = jnp.minimum(jnp.sum(jnp.where(before, row[None, :], 0), axis=1), MICRO - 1)
     slot = jnp.sum(jnp.where(before, column[None, :], 0), axis=1)
-    z, y, c = split_peer(peer)
+    x, y, z, c = place_of(section, peer)
+    near_z = (z + 8 - jnp.where(x == 0, 1, 0)) % 8 // 4
     from_z, from_y, from_c = split_peer(index)
     turn = (y - from_y + ROWS_Y) % ROWS_Y
+    order = jnp.asarray([dy for dy, dc in SLOTS if dc == 0], jnp.int32)
     place = jnp.sum(
         jnp.where(
-            turn[:, None] == jnp.asarray([4, 3, 5, 2, 6, 1, 7, 0], jnp.int32)[None, :],
-            jnp.arange(ROWS_Y, dtype=jnp.int32)[None, :],
-            0,
+            turn[:, None] == order[None, :], jnp.arange(ROWS_Y, dtype=jnp.int32)[None, :], 0
         ),
         axis=1,
     )
-    step = place * 4 + jnp.where(from_z == z, 2, 0) + jnp.where(from_c == c, 0, 1)
+    step = place * 2 + jnp.where(from_z == near_z, FAR, 0) + jnp.where(from_c == c, 0, 1)
     here = (jnp.arange(CAP, dtype=jnp.int32)[:, None] == slot[None, :]) & (column[None, :] > 0)
     source = jnp.sum(jnp.where(here, step[None, :], 0), axis=1)
     taken = jnp.sum(here.astype(jnp.int32), axis=1)

time: 180 us -> 153 us (0.85)
  the two profiles are of different devices: /device:TPU:193 before, /device:TPU:1 now
where the time goes in v2:
time: 153 us; the launch traced here: 152 us
  Pallas kernels  145 us (95%)
  local copies, waits for them, and re-layouts  4.97 us (3%)
    pallas_call x1, Pallas kernels, route(): pl.pallas_call(route_kernel, out_shape=(jax.ShapeDtypeStruct(slots, BF),...  110 us
    pallas_call x1, Pallas kernels, reduce_terms(): pl.pallas_call(reduce_kernel, out_shape=jax.ShapeDtypeStruct((2 * HALF, W...  23.8 us
    pallas_call x1, Pallas kernels, section_step(): pl.pallas_call(section_kernel, out_shape=(jax.ShapeDtypeStruct((TOK, D),...  11.4 us
    unnamed x10, local copies, waits for them, and re-layouts  4.06 us

profile of v2, /device:TPU:1, one launch (start us, length us, event | category | flops | bytes accessed | tf_op | source)
XLA Modules:
  0.0 152.3 jit_solution(12872063967351594750)
XLA Ops:
  0.6 0.0 copy-start
  0.6 0.0 copy-start.1
  0.8 0.8 copy-done
  1.6 0.2 dynamic-slice_reduce_fusion
  1.8 0.1 select_reduce_fusion
  1.9 0.7 select_reduce_fusion.3
  2.7 0.1 select_reduce_fusion.1
  2.8 0.1 convert_reduce_fusion
  2.9 0.0 copy-start.2
  2.9 1.3 copy-done.2
  4.2 0.0 copy-start.3
  4.2 1.0 copy-done.3
  5.2 0.0 copy-start.4
  5.2 1.0 copy-done.4
  6.2 110.1 %route.1 = (bf16[32,8,5120]{2,1,0:T(8,128)(2,1)S(1)}, bf16[2,2,16,5120]{3,2,1,0:T(8,128)(2,1)S(1)}) custom-call(s32[32]{0:T(128)S(1)} %broadcast_minimum_fusion.pick, bf16[16,8,5120]{2,1,0:T(8,128)(2,1)S(1)} %bitcast.10, bf16[2,16,5120]{2,1,0:T(8,128)(2,1)S(1)} %bitcast.11, bf16[2,16,5120]{2,1,0:T(8,128)(2,1)S(1)} %bitcast.12), custom_call_target="tpu_custom_call" | custom-call | tf_op jit(solution)/shard_map/route/pallas_call | solution.py:200
  116.3 0.0 copy-done.1
  116.3 11.4 %section_step.1 = (bf16[160,5120]{1,0:T(8,128)(2,1)}, f32[64,5120]{1,0:T(8,128)S(1)}) custom-call(s32[20]{0:T(128)S(1)} %get-tuple-element.12.source, s32[20]{0:T(128)S(1)} %get-tuple-element.11.taken, bf16[32,8,5120]{2,1,0:T(8,128)(2,1)S(1)} %get-tuple-element.7.arrived, bf16[160,5120]{1,0:T(8,128)(2,1)S(1)} %bitcast.9, ...), custom_call_target="tpu_custom_call" | custom-call | tf_op jit(solution)/shard_map/section_step/pallas_call | solution.py:318
  127.8 23.8 %reduce_terms.1 = f32[64,384]{1,0:T(8,128)S(1)} custom-call(f32[64,5120]{1,0:T(8,128)S(1)} %get-tuple-element.10.terms), custom_call_target="tpu_custom_call" | custom-call | tf_op jit(solution)/shard_map/reduce_terms/pallas_call | solution.py:419
  151.5 0.7 fusion.8
  (5 shorter events, 0.0 us)
Async XLA Ops:
  0.6 1.0 copy-start
  0.6 115.7 %copy-start.1 = (bf16[1,1,160,5120]{3,2,1,0:T(8,128)(2,1)S(1)}, bf16[1,1,160,5120]{3,2,1,0:T(8,128)(2,1)}, u32[]{:S(2)}) copy-start(bf16[1,1,160,5120]{3,2,1,0:T(8,128)(2,1)} %param.10) | copy-start | bytes 4915204
  2.9 1.3 copy-start.2
  4.2 1.0 copy-start.3
  5.2 1.0 copy-start.4

commit v3 on v2

--- a/solution.py
+++ b/solution.py
@@ -18,8 +18,8 @@
 MICRO = 16
 CAP = 20
 TOK = CAP * MB
-BLOCK = 32
-CHUNK = 1024
+BLOCK = 160
+CHUNK = 256
 WINDOW = 384
 epsilon = 1e-06
 
@@ -122,11 +122,6 @@
         else:
             final[i].start()
 
-    @pl.when(leaving)
-    def _():
-        for k in range(SPLIT):
-            outward[k].start()
-
     for k in range(FAR):
         if k < SPLIT:
 
@@ -136,7 +131,13 @@
         else:
             far[k].start()
         near[k].start()
-        if k == FAR // 2:
+        if k < SPLIT:
+
+            @pl.when(leaving)
+            def _():
+                outward[k].start()
+
+        if k == FAR - 3:
 
             @pl.when(c == 0)
             def _():
@@ -159,7 +160,7 @@
             def _():
                 outward[t].wait_recv()
                 onward[t].start()
-        if t == FAR - 2:
+        if t == FAR:
             weight_hop(w_in).wait_recv()
             share.start()
         if t >= LAG:
@@ -228,6 +229,18 @@
     )(pick, inbox, w_in, w_out)
 
 
+def split_peer(peer):
+    return peer // 16, (peer // 2) % ROWS_Y, peer % 2
+
+
+def join_peer(z, y, c):
+    return z * 16 + y * 2 + c
+
+
+HALF = 2 * RANK
+SPREAD = [(dy, dz) for dy in (4, 3, 5, 2, 6, 1, 7, 0) for dz in (1, 0)]
+
+
 def across(left, right):
     return lax.dot_general(left, right, (((1,), (1,)), ((), ())), preferred_element_type=F32)
 
@@ -245,8 +258,27 @@
 
 
 def section_kernel(
-    source, taken, arrived, returned, weights, handed, terms, hid, n0, n1, g1, l0, l1, b0, b1
+    source, taken, arrived, returned, weights, handed, total, hid, n0, n1, g1, l0, l1, b0, b1,
+    terms, half, other_half, summed, landed, own, other, ss, rs, sc, rc
 ):
+    section = lax.axis_index("section")
+    z, y, c = split_peer(lax.axis_index("peer"))
+    ahead = (section + 1) % SECTIONS
+    behind = (section + SECTIONS - 1) % SECTIONS
+    partner = (section, join_peer(z, y, 1 - c))
+    mine = pl.ds(pl.multiple_of(c * HALF, HALF), HALF)
+    theirs = pl.ds(pl.multiple_of((1 - c) * HALF, HALF), HALF)
+
+    barrier = pltpu.get_barrier_semaphore()
+    pl.semaphore_signal(barrier, inc=1, device_id=partner, device_id_type=MESH)
+    for dy, dz in SPREAD:
+        pl.semaphore_signal(
+            barrier,
+            inc=1,
+            device_id=(ahead, join_peer((z + dz) % 2, (y + dy) % ROWS_Y, c)),
+            device_id_type=MESH,
+        )
+
     pieces = [pl.ds(k, CHUNK) for k in range(0, D, CHUNK)]
 
     def block(step, carry):
@@ -257,7 +289,7 @@
             for k in range(BLOCK // MB):
                 slot = step * (BLOCK // MB) + k
                 part = arrived[source[slot], :, piece].astype(F32)
-                parts.append(jnp.where(taken[slot] > 0, part, 0.0))
+                parts.append(part * taken[slot])
             x = jnp.concatenate(parts, axis=0)
             hid[:, piece] = x
             square += jnp.sum(x * x, axis=-1, keepdims=True)
@@ -305,11 +337,69 @@
         return carry
 
     lax.fori_loop(0, TOK // BLOCK, block, 0)
-    for piece in pieces:
-        terms[0:16, piece] = down(b0[...], n0[:, piece])
-        terms[16:32, piece] = down(b1[...], n1[:, piece])
-        terms[32:48, piece] = down(l0[...], g1[:, piece])
-        terms[48:64, piece] = down(l1[...], returned[:, piece])
+    def fill(dz, first, last):
+        for k in range(first, last, CHUNK):
+            piece = pl.ds(pl.multiple_of((z + dz) % 2 * (D // 2) + k, CHUNK), CHUNK)
+            terms[0:16, piece] = down(b0[...], n0[:, piece])
+            terms[16:32, piece] = down(b1[...], n1[:, piece])
+            terms[32:48, piece] = down(l0[...], g1[:, piece])
+            terms[48:64, piece] = down(l1[...], returned[:, piece])
+            half[:, piece] = terms[theirs, piece].astype(BF)
+
+    swaps = []
+    for dz in (1, 0):
+        columns = pl.ds(pl.multiple_of((z + dz) % 2 * (D // 2), D // 2), D // 2)
+        swap = pltpu.make_async_remote_copy(
+            src_ref=half.at[:, columns],
+            dst_ref=other_half.at[:, columns],
+            send_sem=sc.at[1 + dz],
+            recv_sem=rc.at[1 + dz],
+            device_id=partner,
+            device_id_type=MESH,
+        )
+        swaps.append((dz, columns, swap))
+    fill(1, 0, D // 2)
+    pl.semaphore_wait(barrier, 1 + len(SPREAD))
+    fill(0, 0, CHUNK)
+    swaps[0][2].start()
+    fill(0, CHUNK, D // 2)
+    swaps[1][2].start()
+    copies = []
+    for dz, columns, swap in swaps:
+        swap.wait_recv()
+        summed[:, columns] = (terms[mine, columns] + other_half[:, columns].astype(F32)).astype(BF)
+        for i, (dy, turn) in enumerate(SPREAD):
+            if turn != dz:
+                continue
+            chip_z, chip_y = (z + dz) % 2, (y + dy) % ROWS_Y
+            start = pl.multiple_of(128 * ((5 * (chip_z * ROWS_Y + chip_y)) // 2), 128)
+            copy = pltpu.make_async_remote_copy(
+                src_ref=summed.at[:, pl.ds(start, WINDOW)],
+                dst_ref=landed.at[i],
+                send_sem=ss.at[i],
+                recv_sem=rs.at[i],
+                device_id=(behind, join_peer(chip_z, chip_y, c)),
+                device_id_type=MESH,
+            )
+            copy.start()
+            copies.append(copy)
+    for _, _, swap in swaps:
+        swap.wait_send()
+    for copy in copies:
+        copy.wait()
+    own[...] = jnp.sum(landed[...].astype(F32), axis=0)
+    back = pltpu.make_async_remote_copy(
+        src_ref=own,
+        dst_ref=other,
+        send_sem=sc.at[0],
+        recv_sem=rc.at[0],
+        device_id=partner,
+        device_id_type=MESH,
+    )
+    back.start()
+    back.wait()
+    total[mine, :] = own[...] / PEERS
+    total[theirs, :] = other[...] / PEERS
 
 
 def section_step(source, taken, arrived, returned, weights):
@@ -319,7 +409,7 @@
         section_kernel,
         out_shape=(
             jax.ShapeDtypeStruct((TOK, D), BF),
-            jax.ShapeDtypeStruct((4 * RANK, D), F32),
+            jax.ShapeDtypeStruct((2 * HALF, WINDOW), F32),
         ),
         in_specs=[smem, smem, vmem, vmem, vmem],
         out_specs=(vmem, vmem),
@@ -332,112 +422,23 @@
             pltpu.VMEM((TOK, RANK), BF),
             pltpu.VMEM((TOK, RANK), BF),
             pltpu.VMEM((TOK, RANK), BF),
-        ],
-        compiler_params=pltpu.CompilerParams(vmem_limit_bytes=40 << 20),
-        name="section_step",
-    )(source, taken, arrived, returned, weights)
-
-
-def split_peer(peer):
-    return peer // 16, (peer // 2) % ROWS_Y, peer % 2
-
-
-def join_peer(z, y, c):
-    return z * 16 + y * 2 + c
-
-
-HALF = 2 * RANK
-SPREAD = [(dy, dz) for dy in (4, 3, 5, 2, 6, 1, 7, 0) for dz in (1, 0)]
-
-
-def reduce_kernel(terms, total, half, other_half, summed, landed, own, other, ss, rs, sc, rc):
-    section = lax.axis_index("section")
-    z, y, c = split_peer(lax.axis_index("peer"))
-    ahead = (section + 1) % SECTIONS
-    behind = (section + SECTIONS - 1) % SECTIONS
-    partner = (section, join_peer(z, y, 1 - c))
-    mine = pl.ds(pl.multiple_of(c * HALF, HALF), HALF)
-    theirs = pl.ds(pl.multiple_of((1 - c) * HALF, HALF), HALF)
-
-    barrier = pltpu.get_barrier_semaphore()
-    pl.semaphore_signal(barrier, inc=1, device_id=partner, device_id_type=MESH)
-    for dy, dz in SPREAD:
-        pl.semaphore_signal(
-            barrier,
-            inc=1,
-            device_id=(ahead, join_peer((z + dz) % 2, (y + dy) % ROWS_Y, c)),
-            device_id_type=MESH,
-        )
-    half[...] = terms[theirs, :].astype(BF)
-    pl.semaphore_wait(barrier, 1 + len(SPREAD))
-
-    to_core = pltpu.make_async_remote_copy(
-        src_ref=half,
-        dst_ref=other_half,
-        send_sem=sc.at[0],
-        recv_sem=rc.at[0],
-        device_id=partner,
-        device_id_type=MESH,
-    )
-    to_core.start()
-    to_core.wait()
-    summed[...] = (terms[mine, :] + other_half[...].astype(F32)).astype(BF)
-    copies = []
-    for i, (dy, dz) in enumerate(SPREAD):
-        chip_z, chip_y = (z + dz) % 2, (y + dy) % ROWS_Y
-        start = pl.multiple_of(128 * ((5 * (chip_z * ROWS_Y + chip_y)) // 2), 128)
-        copy = pltpu.make_async_remote_copy(
-            src_ref=summed.at[:, pl.ds(start, WINDOW)],
-            dst_ref=landed.at[i],
-            send_sem=ss.at[i],
-            recv_sem=rs.at[i],
-            device_id=(behind, join_peer(chip_z, chip_y, c)),
-            device_id_type=MESH,
-        )
-        copy.start()
-        copies.append(copy)
-    for copy in copies:
-        copy.wait()
-    own[...] = jnp.sum(landed[...].astype(F32), axis=0)
-    back = pltpu.make_async_remote_copy(
-        src_ref=own,
-        dst_ref=other,
-        send_sem=sc.at[1],
-        recv_sem=rc.at[1],
-        device_id=partner,
-        device_id_type=MESH,
-    )
-    back.start()
-    back.wait()
-    total[mine, :] = own[...] / PEERS
-    total[theirs, :] = other[...] / PEERS
-
-
-def reduce_terms(terms):
-    vmem = pl.BlockSpec(memory_space=pltpu.VMEM)
-    count = len(SPREAD)
-    return pl.pallas_call(
-        reduce_kernel,
-        out_shape=jax.ShapeDtypeStruct((2 * HALF, WINDOW), F32),
-        in_specs=[vmem],
-        out_specs=vmem,
-        scratch_shapes=[
+            pltpu.VMEM((2 * HALF, D), F32),
             pltpu.VMEM((HALF, D), BF),
             pltpu.VMEM((HALF, D), BF),
             pltpu.VMEM((HALF, D), BF),
-            pltpu.VMEM((count, HALF, WINDOW), BF),
+            pltpu.VMEM((len(SPREAD), HALF, WINDOW), BF),
             pltpu.VMEM((HALF, WINDOW), F32),
             pltpu.VMEM((HALF, WINDOW), F32),
-            pltpu.SemaphoreType.DMA((count,)),
-            pltpu.SemaphoreType.DMA((count,)),
-            pltpu.SemaphoreType.DMA((2,)),
-            pltpu.SemaphoreType.DMA((2,)),
+            pltpu.SemaphoreType.DMA((len(SPREAD),)),
+            pltpu.SemaphoreType.DMA((len(SPREAD),)),
+            pltpu.SemaphoreType.DMA((3,)),
+            pltpu.SemaphoreType.DMA((3,)),
         ],
         compiler_params=pltpu.CompilerParams(
-            collective_id=1, has_side_effects=True, vmem_limit_bytes=32 << 20
-        ),
-        name="reduce_terms",
-    )(terms)
+            collective_id=1, has_side_effects=True, vmem_limit_bytes=40 << 20
+        ),
+        name="section_step",
+    )(source, taken, arrived, returned, weights)
 
 
 def tables(routes, section, peer):
@@ -466,7 +467,7 @@
     step = place * 2 + jnp.where(from_z == near_z, FAR, 0) + jnp.where(from_c == c, 0, 1)
     here = (jnp.arange(CAP, dtype=jnp.int32)[:, None] == slot[None, :]) & (column[None, :] > 0)
     source = jnp.sum(jnp.where(here, step[None, :], 0), axis=1)
-    taken = jnp.sum(here.astype(jnp.int32), axis=1)
+    taken = jnp.sum(here.astype(F32), axis=1)
     return pick, source, taken
 
 
@@ -477,8 +478,7 @@
     arrived, weights = route(
         pick, inbox.reshape(MICRO, MB, D), adapter_in[0], adapter_out[0]
     )
-    handed, terms = section_step(source, taken, arrived, returned[0, 0], weights)
-    total = reduce_terms(terms)
+    handed, total = section_step(source, taken, arrived, returned[0, 0], weights)
     start = (peer // 2 % 2) * 64 + (peer % 2) * 160
     own = lax.dynamic_slice_in_dim(total, start, D // PEERS, axis=1).reshape(2, 2, RANK, D // PEERS)
     return handed[None, None], own[0][None], own[1][None]

time: 153 us -> 144 us (0.941)
  the two profiles are of different devices: /device:TPU:1 before, /device:TPU:7 now
where the time goes in v3:
time: 144 us
  Pallas kernels  136 us (94%)
  local copies, waits for them, and re-layouts  6.14 us (4%)
    pallas_call x1, Pallas kernels, route(): pl.pallas_call(route_kernel, out_shape=(jax.ShapeDtypeStruct(slots, BF),...  105 us
    pallas_call x1, Pallas kernels, section_step(): pl.pallas_call(section_kernel, out_shape=(jax.ShapeDtypeStruct((TOK, D),...  30.9 us
    unnamed x11, local copies, waits for them, and re-layouts  5.23 us

profile of v3, /device:TPU:7, one launch (start us, length us, event | category | flops | bytes accessed | tf_op | source)
XLA Modules:
  0.0 143.9 jit_solution(9070749194205163217)
XLA Ops:
  0.6 0.0 copy-start
  0.6 0.0 copy-start.1
  0.8 0.8 copy-done
  1.6 0.2 dynamic-slice_reduce_fusion
  1.8 0.1 select_reduce_fusion
  1.9 0.7 select_reduce_fusion.3
  2.7 0.1 select_reduce_fusion.1
  2.8 0.1 select_reduce_fusion.2.source
  2.9 0.1 convert_reduce_fusion.taken
  3.0 0.0 copy-start.2
  3.0 1.3 copy-done.2
  4.4 0.0 copy-start.3
  4.4 1.0 copy-done.3
  5.3 0.0 copy-start.4
  5.3 1.0 copy-done.4
  6.3 104.8 %route.1 = (bf16[32,8,5120]{2,1,0:T(8,128)(2,1)S(1)}, bf16[2,2,16,5120]{3,2,1,0:T(8,128)(2,1)S(1)}) custom-call(s32[32]{0:T(128)S(1)} %broadcast_minimum_fusion.pick, bf16[16,8,5120]{2,1,0:T(8,128)(2,1)S(1)} %bitcast.11, bf16[2,16,5120]{2,1,0:T(8,128)(2,1)S(1)} %bitcast.12, bf16[2,16,5120]{2,1,0:T(8,128)(2,1)S(1)} %bitcast.13), custom_call_target="tpu_custom_call" | custom-call | tf_op jit(solution)/shard_map/route/pallas_call | solution.py:201
  111.1 0.0 copy-done.1
  111.1 30.9 %section_step.1 = (bf16[160,5120]{1,0:T(8,128)(2,1)S(1)}, f32[64,384]{1,0:T(8,128)S(1)}) custom-call(s32[20]{0:T(128)S(1)} %select_reduce_fusion.2.source, f32[20]{0:T(128)S(1)} %convert_reduce_fusion.taken, bf16[32,8,5120]{2,1,0:T(8,128)(2,1)S(1)} %get-tuple-element.7.arrived, bf16[160,5120]{1,0:T(8,128)(2,1)S(1)} %bitcast.10, ...), custom_call_target="tpu_custom_call" | custom-call | tf_op jit(solution)/shard_map/section_step/pallas_call | solution.py:408
  142.0 0.7 fusion.8
  142.7 1.2 copy.10
  (5 shorter events, 0.0 us)
Async XLA Ops:
  0.6 1.0 copy-start
  0.6 110.4 %copy-start.1 = (bf16[1,1,160,5120]{3,2,1,0:T(8,128)(2,1)S(1)}, bf16[1,1,160,5120]{3,2,1,0:T(8,128)(2,1)}, u32[]{:S(2)}) copy-start(bf16[1,1,160,5120]{3,2,1,0:T(8,128)(2,1)} %param.10) | copy-start | bytes 4915204
  3.0 1.3 copy-start.2
  4.4 1.0 copy-start.3
  5.3 1.0 copy-start.4

commit v4 on v3

--- a/solution.py
+++ b/solution.py
@@ -131,11 +131,11 @@
         else:
             far[k].start()
         near[k].start()
-        if k < SPLIT:
+        if 2 <= k < 2 + SPLIT:
 
             @pl.when(leaving)
             def _():
-                outward[k].start()
+                outward[k - 2].start()
 
         if k == FAR - 3:
 
@@ -154,12 +154,12 @@
         if t < FAR:
             near[t].wait_recv()
             pass_on(FAR + t)
-        if t < SPLIT:
+        if 2 <= t < 2 + SPLIT:
 
             @pl.when(entering)
             def _():
-                outward[t].wait_recv()
-                onward[t].start()
+                outward[t - 2].wait_recv()
+                onward[t - 2].start()
         if t == FAR:
             weight_hop(w_in).wait_recv()
             share.start()

time: 144 us -> 144 us (level)
  no operation moved by 1% of the time
where the time goes in v4:
time: 144 us
  Pallas kernels  136 us (94%)
  local copies, waits for them, and re-layouts  6.14 us (4%)
    pallas_call x1, Pallas kernels, route(): pl.pallas_call(route_kernel, out_shape=(jax.ShapeDtypeStruct(slots, BF),...  105 us
    pallas_call x1, Pallas kernels, section_step(): pl.pallas_call(section_kernel, out_shape=(jax.ShapeDtypeStruct((TOK, D),...  31 us
    unnamed x11, local copies, waits for them, and re-layouts  5.23 us

profile of v4, /device:TPU:7, one launch (start us, length us, event | category | flops | bytes accessed | tf_op | source)
XLA Modules:
  0.0 144.0 jit_solution(602519523848378152)
XLA Ops:
  0.6 0.0 copy-start
  0.6 0.0 copy-start.1
  0.8 0.8 copy-done
  1.6 0.2 dynamic-slice_reduce_fusion
  1.8 0.1 select_reduce_fusion
  1.9 0.7 select_reduce_fusion.3
  2.7 0.1 select_reduce_fusion.1
  2.8 0.1 select_reduce_fusion.2.source
  2.9 0.1 convert_reduce_fusion.taken
  3.0 0.0 copy-start.2
  3.0 1.3 copy-done.2
  4.4 0.0 copy-start.3
  4.4 1.0 copy-done.3
  5.3 0.0 copy-start.4
  5.3 1.0 copy-done.4
  6.3 104.8 %route.1 = (bf16[32,8,5120]{2,1,0:T(8,128)(2,1)S(1)}, bf16[2,2,16,5120]{3,2,1,0:T(8,128)(2,1)S(1)}) custom-call(s32[32]{0:T(128)S(1)} %broadcast_minimum_fusion.pick, bf16[16,8,5120]{2,1,0:T(8,128)(2,1)S(1)} %bitcast.11, bf16[2,16,5120]{2,1,0:T(8,128)(2,1)S(1)} %bitcast.12, bf16[2,16,5120]{2,1,0:T(8,128)(2,1)S(1)} %bitcast.13), custom_call_target="tpu_custom_call" | custom-call | tf_op jit(solution)/shard_map/route/pallas_call | solution.py:201
  111.1 0.0 copy-done.1
  111.1 31.0 %section_step.1 = (bf16[160,5120]{1,0:T(8,128)(2,1)S(1)}, f32[64,384]{1,0:T(8,128)S(1)}) custom-call(s32[20]{0:T(128)S(1)} %select_reduce_fusion.2.source, f32[20]{0:T(128)S(1)} %convert_reduce_fusion.taken, bf16[32,8,5120]{2,1,0:T(8,128)(2,1)S(1)} %get-tuple-element.7.arrived, bf16[160,5120]{1,0:T(8,128)(2,1)S(1)} %bitcast.10, ...), custom_call_target="tpu_custom_call" | custom-call | tf_op jit(solution)/shard_map/section_step/pallas_call | solution.py:408
  142.1 0.7 fusion.8
  142.8 1.2 copy.10
  (5 shorter events, 0.0 us)
Async XLA Ops:
  0.6 1.0 copy-start
  0.6 110.4 %copy-start.1 = (bf16[1,1,160,5120]{3,2,1,0:T(8,128)(2,1)S(1)}, bf16[1,1,160,5120]{3,2,1,0:T(8,128)(2,1)}, u32[]{:S(2)}) copy-start(bf16[1,1,160,5120]{3,2,1,0:T(8,128)(2,1)} %param.10) | copy-start | bytes 4915204
  3.0 1.3 copy-start.2
  4.4 1.0 copy-start.3
  5.3 1.0 copy-start.4
